TPU v7x, 256 devices: a whole 4x4x8 slice. The times are simulated.
256 devices in a mesh: row: 2 (over core), col: 64 (over z, y, x_hi), layer: 2 (over x_lo).
Axes of the slice: x: 4 (x_hi: 2, x_lo: 2; x = x_hi * 2 + x_lo), y: 4, z: 8, core: 2. Of those that a mesh axis runs over, the one named last changes fastest.
Arguments:
- flow_cols: int32 [16, 2, 64], P('row', 'layer', 'col'), may hold values from 0 to 64, as said below
- flow_vals: bfloat16 [16, 2, 64, 128, 128], P('row', 'layer', 'col'), may hold values from -22 to 22
- window_flow: bfloat16 [2, 8192, 32768], P('layer', 'row', 'col'), may hold values from -0.1403165 to 0.1403165
Outputs:
- flow_next: float32 [2048, 32768], P(('row', 'layer'), 'col')
Inputs may be any that keep to these rules, and one draw needn't show every extreme that they name: `flow_cols`: an entry 64 marks an empty slot; the live entries of one block row and layer are distinct; every block row and layer has at least one live slot, and some block row and layer has all 64 slots live.
All inputs are finite; a program needn't handle non-finite values.
Results may differ from a plain program's by a relative error of at most 0.0003.
Values may be sent and summed in bfloat16 or wider, within the bound.
A program may use at most 128 MiB of HBM per device.

v0:
```python
import jax
import jax.numpy as jnp
from jax import lax
from jax.sharding import PartitionSpec as P


def body(flow_cols, flow_vals, window_flow):
    row = lax.axis_index("row")
    layer = lax.axis_index("layer")
    n_layer = lax.axis_size("layer")
    own_g = window_flow[0]
    half_rows = own_g.shape[0]
    other_g = lax.ppermute(own_g, "row", perm=[(0, 1), (1, 0)])
    panel = jnp.zeros((2 * half_rows, own_g.shape[1]), own_g.dtype)
    panel = lax.dynamic_update_slice_in_dim(panel, own_g, row * half_rows, 0)
    panel = lax.dynamic_update_slice_in_dim(panel, other_g, (1 - row) * half_rows, 0)
    block_size = flow_vals.shape[-1]
    block_count = panel.shape[0] // block_size
    row_blocks = flow_vals.shape[0]
    wide_cols = jnp.broadcast_to(
        flow_cols.astype(jnp.bfloat16)[..., None, None], flow_cols.shape + (16, 128)
    )
    wide_cols = lax.optimization_barrier(wide_cols)
    slot_cols = lax.all_gather(wide_cols, "col", axis=2, tiled=True)[:, 0, :, 0, 0].astype(
        jnp.float32
    )
    slot_vals = lax.all_gather(flow_vals, "col", axis=2, tiled=True)[:, 0]
    column_ids = jnp.arange(block_count, dtype=jnp.float32)
    one_hot = (slot_cols[:, :, None] == column_ids[None, None, :]).astype(jnp.bfloat16)
    share = row_blocks // n_layer
    send_blocks = (1 - layer) * share
    keep_blocks = layer * share

    def expand(first_block):
        vals = lax.dynamic_slice_in_dim(slot_vals, first_block, share, 0)
        hot = lax.dynamic_slice_in_dim(one_hot, first_block, share, 0)
        dense = jnp.einsum("isab,isk->iakb", vals, hot, preferred_element_type=jnp.bfloat16)
        dense = dense.reshape(share * block_size, block_count * block_size)
        return jnp.dot(dense, panel, preferred_element_type=jnp.float32)

    sent = expand(send_blocks)
    received = lax.ppermute(sent, "layer", perm=[(0, 1), (1, 0)])
    summed = expand(keep_blocks) + received
    squares = summed * summed
    total_rows = row_blocks * block_size * lax.axis_size("row")
    column_sums = lax.psum(jnp.sum(squares, axis=0), ("row", "layer"))
    return squares / (column_sums / total_rows + 1e-06)


def solution(mesh):
    placed = (
        P("row", "layer", "col"),
        P("row", "layer", "col", None, None),
        P("layer", "row", "col"),
    )
    return jax.shard_map(
        body, mesh=mesh, in_specs=placed, out_specs=P(("row", "layer"), "col"), check_vma=False
    )
```

profile of v0, /device:TPU:1, one launch (start us, length us, event | category | flops | bytes accessed | tf_op | source)
XLA Modules:
  0.0 435.7 jit_solution(5035930560204560066)
XLA Ops:
  6.5 0.7 convert_bitcast_fusion
  7.2 0.7 broadcast_in_dim.7
  7.9 0.0 all-gather.3.cloned.1.call-update
  7.9 0.0 all-gather.5.cloned.1.call-start
  8.0 0.7 all-gather.5.cloned.1.call-update
  8.7 3.3 collective-permute-start
  12.0 4.2 broadcast_in_dim.16
  16.2 2.2 constant_dynamic-update-slice_fusion.1
  18.4 111.7 %all-gather.3.cloned.1.call-done = bf16[8,1,64,16,128]{4,3,1,0,2:T(8,128)(2,1)} async-done(((bf16[8,1,1,16,128]{4,3,1,0,2:T(8,128)(2,1)}), bf16[8,1,64,16,128]{4,3,1,0,2:T(8,128)(2,1)}) %all-gather.3.cloned.1.call-update) | async-done | bytes 2097168 | tf_op jit(solution)/shard_map/all_gather | solution.py:24
  130.1 1.4 slice.4
  131.5 0.2 copy.14
  131.6 0.1 iota_compare_fusion
  131.7 0.0 collective-permute-done
  131.7 4.4 %constant_dynamic-update-slice_fusion = bf16[8192,512]{1,0:T(8,128)(2,1)} fusion(bf16[8192,512]{1,0:T(8,128)(2,1)} %constant_dynamic-update-slice_fusion.1, bf16[4096,512]{1,0:T(8,128)(2,1)} %collective-permute-done, s32[]{:T(128)S(6)} %select_n.16), kind=kLoop, calls=%fused_computation.24 | loop fusion | bytes 8388612 | tf_op jit(solution)/shard_map/dynamic_update_slice | solution.py:16
  136.1 209.0 %all-gather.5.cloned.1.call-done = bf16[8,1,64,128,128]{4,3,2,1,0:T(8,128)(2,1)} async-done(((bf16[8,1,1,128,128]{4,3,2,1,0:T(8,128)(2,1)}), bf16[8,1,64,128,128]{4,3,2,1,0:T(8,128)(2,1)}) %all-gather.5.cloned.1.call-update) | async-done | bytes 16777232 | tf_op jit(solution)/shard_map/all_gather | solution.py:27
  345.1 9.4 %constant_dynamic-slice_fusion.1 = (bf16[4,1,64,128,128]{4,3,2,1,0:T(8,128)(2,1)S(1)}, bf16[4,1,64,128,128]{4,3,2,1,0:T(8,128)(2,1)}) fusion(bf16[8,1,64,128,128]{4,3,2,1,0:T(8,128)(2,1)} %all-gather.5.cloned.1.call-done, s32[]{:T(128)S(6)} %select_n.14, s32[]{:T(128)S(6)} %select_n.17), kind=kLoop, calls=%fused_computation.26 | loop fusion | bytes 33554440 | tf_op jit(solution)/shard_map/dynamic_slice | solution.py:35
  354.6 13.4 %fusion.6 = bf16[4,64,128,128]{3,1,2,0:T(8,128)(2,1)} fusion(bf16[4,1,64,128,128]{4,3,2,1,0:T(8,128)(2,1)} %get-tuple-element.6, pred[8,64,64]{1,2,0:T(32,128)(4,1)S(1)} %iota_compare_fusion, s32[]{:T(128)S(6)} %select_n.17), kind=kOutput, calls=%fused_computation.6 | convolution fusion | flops 536870912 | bytes 16809988 | tf_op jit(solution)/shard_map/isab,isk->iakb/dot_general | solution.py:37
  368.0 13.8 %fusion = f32[512,512]{1,0:T(8,128)S(1)} fusion(bf16[8192,512]{1,0:T(8,128)(2,1)} %constant_dynamic-update-slice_fusion, bf16[64,8,64,128]{3,2,1,0:T(8,128)(2,1)} %bitcast.44), kind=kOutput, calls=%fused_computation | convolution fusion | flops 4294967296 | bytes 17825792 | tf_op jit(solution)/shard_map/dot_general | solution.py:39
  381.8 0.4 collective-permute-start.1
  382.2 8.4 %fusion.8 = bf16[4,64,128,128]{3,1,2,0:T(8,128)(2,1)} fusion(bf16[4,1,64,128,128]{4,3,2,1,0:T(8,128)(2,1)S(1)} %get-tuple-element.5, pred[8,64,64]{1,2,0:T(32,128)(4,1)S(1)} %iota_compare_fusion, s32[]{:T(128)S(6)} %select_n.14), kind=kOutput, calls=%fused_computation.8 | convolution fusion | flops 536870912 | bytes 16809988 | tf_op jit(solution)/shard_map/isab,isk->iakb/dot_general | solution.py:37
  390.6 14.9 %collective-permute-done.1 = f32[512,512]{1,0:T(8,128)S(1)} collective-permute-done((f32[512,512]{1,0:T(8,128)S(1)}, f32[512,512]{1,0:T(8,128)S(1)}, u32[]{:S(2)}, u32[]{:S(2)}) %collective-permute-start.1) | collective-permute-done | bytes 1048608 | tf_op jit(solution)/shard_map/ppermute | solution.py:42
  405.5 13.8 %fusion.24 = (f32[512]{0:T(512)S(1)}, f32[512,512]{1,0:T(8,128)S(1)}) fusion(f32[512,512]{1,0:T(8,128)S(1)} %collective-permute-done.1, bf16[8192,512]{1,0:T(8,128)(2,1)} %constant_dynamic-update-slice_fusion, bf16[64,8,64,128]{3,2,1,0:T(8,128)(2,1)} %bitcast.43), kind=kOutput, calls=%fused_computation.29 | convolution fusion | flops 4295753216 | bytes 18876416 | tf_op jit(solution)/shard_map/dot_general | solution.py:39
  419.3 8.4 %psum.7 = f32[512]{0:T(512)S(1)} all-reduce(f32[512]{0:T(512)S(1)} %get-tuple-element.7), channel_id=1, replica_groups=mesh['row'=2,'col'=64,'layer'=2] {'row','layer'}, use_global_device_ids=true, to_apply=%region_1.0 | all-reduce | flops 512 | bytes 4096 | tf_op jit(solution)/shard_map/psum | solution.py:46
  427.7 1.1 broadcast_divide_fusion
  (5 shorter events, 0.0 us)
Async XLA Ops:
  6.5 123.5 %all-gather.3.cloned.1.call-start = ((), (), s32[]{:S(2)}) async-start(), calls=%async_computation | async-start | bytes 2129920 | tf_op jit(solution)/shard_map/all_gather | solution.py:24
  7.9 337.2 %all-gather.5.cloned.1.call-start = ((), (), s32[]{:S(2)}) async-start(), calls=%async_computation.1 | async-start | bytes 17039360 | tf_op jit(solution)/shard_map/all_gather | solution.py:27
  8.7 123.0 %collective-permute-start = (bf16[4096,512]{1,0:T(8,128)(2,1)}, bf16[4096,512]{1,0:T(8,128)(2,1)}, u32[]{:S(2)}, u32[]{:S(2)}) collective-permute-start(bf16[4096,512]{1,0:T(8,128)(2,1)} %bitcast.45), channel_id=1, source_target_pairs={{0,128},{128,0},{1,129},{129,1},{2,130},{130,2},{3,131},{131,3},{4... | collective-permute-start | bytes 12582920 | tf_op jit(solution)/shard_map/ppermute | solution.py:13
  12.0 4.2 copy-start
  381.8 23.7 %collective-permute-start.1 = (f32[512,512]{1,0:T(8,128)S(1)}, f32[512,512]{1,0:T(8,128)S(1)}, u32[]{:S(2)}, u32[]{:S(2)}) collective-permute-start(f32[512,512]{1,0:T(8,128)S(1)} %fusion), channel_id=1, source_target_pairs={{0,1},{1,0},{2,3},{3,2},{4,5},{5,4},{6,7},{7,6},{8,9},{9,8},{10,11... | collective-permute-start | bytes 3145736 | tf_op jit(solution)/shard_map/ppermute | solution.py:42
Sparse Core Ops, SparseCore 0:
  10.9 119.0 all-gather.2
  133.6 211.5 all-gather.4
where the time goes:
time: 436 us
  waiting for transfers between devices  336 us (77%)
  matrix products  49.5 us (11%)
  local copies, waits for them, and re-layouts  22.5 us (5%)
  between operations  13.4 us (3%)
  blocking collectives  8.44 us (2%)
    all_gather x1, waiting for transfers between devices, body(): slot_vals = lax.all_gather(flow_vals, 'col', axis=2, tiled=True)[:, 0]  209 us
    all_gather x1, waiting for transfers between devices, body(): lax.all_gather(wide_cols, 'col', axis=2, tiled=True)[:, 0, :, 0, 0]  112 us
    dot_general x2, matrix products, expand(): return jnp.dot(dense, panel, preferred_element_type=jnp.float32)  27.6 us
    dot_general x2, matrix products, expand(): jnp.einsum('isab,isk->iakb', vals, hot, preferred_element_type=jnp.bfloat16)  21.9 us
    ppermute x1, waiting for transfers between devices, body(): received = lax.ppermute(sent, 'layer', perm=[(0, 1), (1, 0)])  14.9 us
    dynamic_slice x1, local copies, waits for them, and re-layouts, expand(): vals = lax.dynamic_slice_in_dim(slot_vals, first_block, share, 0)  9.42 us
  transfers between devices with their start and end apart: 4, of which 3 were waited for; matrix products, arithmetic and copies ran while one was open for 5% of the time, Pallas kernels for 0%

commit v1 on v0

--- a/solution.py
+++ b/solution.py
@@ -24,7 +24,9 @@
     slot_cols = lax.all_gather(wide_cols, "col", axis=2, tiled=True)[:, 0, :, 0, 0].astype(
         jnp.float32
     )
-    slot_vals = lax.all_gather(flow_vals, "col", axis=2, tiled=True)[:, 0]
+    slot_vals = jnp.concatenate(
+        lax.all_to_all(jnp.stack([flow_vals] * lax.axis_size("col")), "col", 0, 0), axis=2
+    )[:, 0]
     column_ids = jnp.arange(block_count, dtype=jnp.float32)
     one_hot = (slot_cols[:, :, None] == column_ids[None, None, :]).astype(jnp.bfloat16)
     share = row_blocks // n_layer

time: 436 us -> 512 us (1.17)
  waiting for transfers between devices: 336 us -> 387 us
  starting transfers between devices: 3.75 us -> 18.1 us
  local copies, waits for them, and re-layouts: 22.5 us -> 29.5 us
    all_gather x1 -> x0, waiting for transfers between devices: 209 us -> none  [body(): slot_vals = lax.all_gather(flow_vals, 'col', axis=2, tiled=True)[:, 0]]
    all_gather x1, waiting for transfers between devices: 112 us -> 253 us  [body(): lax.all_gather(wide_cols, 'col', axis=2, tiled=True)[:, 0, :, 0, 0]]
    all_to_all x0 -> x1, waiting for transfers between devices: none -> 120 us  [body(): lax.all_to_all(jnp.stack([flow_vals] * lax.axis_size('col')), 'col', 0, 0)]
    another operation x0 -> x2, local copies, waits for them, and re-layouts: none -> 16.4 us
    all_to_all x0 -> x1, starting transfers between devices: none -> 15.5 us  [body(): lax.all_to_all(jnp.stack([flow_vals] * lax.axis_size('col')), 'col', 0, 0)]
    dynamic_slice x1 -> x0, local copies, waits for them, and re-layouts: 9.42 us -> none  [expand(): vals = lax.dynamic_slice_in_dim(slot_vals, first_block, share, 0)]
  transfers between devices with their start and end apart: 4 -> 4, of which waited for: 3 -> 3; matrix products, arithmetic and copies ran while one was open for 5% -> 4% of each run, Pallas kernels for 0% -> 0%
where the time goes in v1:
time: 512 us; the launch traced here: 509 us
  waiting for transfers between devices  387 us (76%)
  matrix products  49.5 us (10%)
  local copies, waits for them, and re-layouts  29.5 us (6%)
  starting transfers between devices  18.1 us (4%)
  between operations  13.5 us (3%)
  blocking collectives  10.4 us (2%)
    all_gather x1, waiting for transfers between devices, body(): lax.all_gather(wide_cols, 'col', axis=2, tiled=True)[:, 0, :, 0, 0]  253 us
    all_to_all x1, waiting for transfers between devices, body(): lax.all_to_all(jnp.stack([flow_vals] * lax.axis_size('col')), 'col', 0, 0)  120 us
    dot_general x2, matrix products, expand(): return jnp.dot(dense, panel, preferred_element_type=jnp.float32)  27.6 us
    dot_general x2, matrix products, expand(): jnp.einsum('isab,isk->iakb', vals, hot, preferred_element_type=jnp.bfloat16)  21.9 us
    all_to_all x1, starting transfers between devices, body(): lax.all_to_all(jnp.stack([flow_vals] * lax.axis_size('col')), 'col', 0, 0)  15.5 us
    ppermute x1, waiting for transfers between devices, body(): received = lax.ppermute(sent, 'layer', perm=[(0, 1), (1, 0)])  12.9 us
    psum x1, blocking collectives, body(): column_sums = lax.psum(jnp.sum(squares, axis=0), ('row', 'layer'))  10.4 us
  transfers between devices with their start and end apart: 4, of which 3 were waited for; matrix products, arithmetic and copies ran while one was open for 4% of the time, Pallas kernels for 0%

profile of v1, /device:TPU:1, one launch (start us, length us, event | category | flops | bytes accessed | tf_op | source)
XLA Modules:
  0.0 508.7 jit_solution(9646576779558340475)
XLA Ops:
  6.5 6.9 %stack.2 = bf16[64,8,1,1,128,128]{5,4,1,3,2,0:T(8,128)(2,1)} broadcast(bf16[8,128,128]{2,1,0:T(8,128)(2,1)} %bitcast.51), dimensions={1,4,5} | broadcast | bytes 17039360 | tf_op jit(solution)/shard_map/stack | solution.py:28
  13.5 15.5 %all-to-all-start = ((bf16[64,8,1,1,128,128]{5,4,1,3,2,0:T(8,128)(2,1)}), bf16[64,8,1,1,128,128]{5,4,1,3,2,0:T(8,128)(2,1)}, u32[]{:S(2)}, u32[]{:S(2)}) async-start(bf16[64,8,1,1,128,128]{5,4,1,3,2,0:T(8,128)(2,1)} %stack.2), calls=%async_computation | async-start | bytes 33554432 | tf_op jit(solution)/shard_map/all_to_all | solution.py:28
  29.0 0.0 all-gather.2.cloned.1.call-start
  29.0 0.7 broadcast_in_dim.7
  29.7 0.0 all-gather.2.cloned.1.call-update
  29.8 1.0 collective-permute-start
  30.8 4.2 broadcast_in_dim.16
  35.0 2.2 constant_dynamic-update-slice_fusion.1
  37.2 253.2 %all-gather.2.cloned.1.call-done = bf16[8,1,64,16,128]{4,3,1,0,2:T(8,128)(2,1)} async-done(((bf16[8,1,1,16,128]{4,3,1,0,2:T(8,128)(2,1)}), bf16[8,1,64,16,128]{4,3,1,0,2:T(8,128)(2,1)}) %all-gather.2.cloned.1.call-update) | async-done | bytes 2097168 | tf_op jit(solution)/shard_map/all_gather | solution.py:24
  290.5 1.4 slice.4
  291.9 0.2 copy.12
  292.0 0.1 iota_compare_fusion
  292.1 0.0 collective-permute-done
  292.1 4.5 constant_dynamic-update-slice_fusion
  296.6 120.4 %all-to-all-done = bf16[64,8,1,1,128,128]{5,4,1,3,2,0:T(8,128)(2,1)} async-done(((bf16[64,8,1,1,128,128]{5,4,1,3,2,0:T(8,128)(2,1)}), bf16[64,8,1,1,128,128]{5,4,1,3,2,0:T(8,128)(2,1)}, u32[]{:S(2)}, u32[]{:S(2)}) %all-to-all-start) | async-done | bytes 16777248 | tf_op jit(solution)/shard_map/all_to_all | solution.py:28
  417.0 9.4 %constant_dynamic-slice_fusion.1 = (bf16[64,4,1,1,128,128]{5,4,1,3,2,0:T(8,128)(2,1)S(1)}, bf16[64,4,1,1,128,128]{5,4,1,3,2,0:T(8,128)(2,1)}) fusion(bf16[64,8,1,1,128,128]{5,4,1,3,2,0:T(8,128)(2,1)} %all-to-all-done, s32[]{:T(128)S(6)} %select_n.14, s32[]{:T(128)S(6)} %select_n.17), kind=kLoop, calls=%fused_computation.24 | loop fusion | bytes 33554440 | tf_op jit(solution)/shard_map/dynamic-slice.2
  426.4 13.4 %fusion.6 = bf16[4,64,128,128]{3,1,2,0:T(8,128)(2,1)} fusion(bf16[64,4,1,1,128,128]{5,4,1,3,2,0:T(8,128)(2,1)} %get-tuple-element.6, pred[8,64,64]{1,2,0:T(32,128)(4,1)S(1)} %iota_compare_fusion, s32[]{:T(128)S(6)} %select_n.17), kind=kOutput, calls=%fused_computation.7 | convolution fusion | flops 536870912 | bytes 16809988 | tf_op jit(solution)/shard_map/isab,isk->iakb/dot_general | solution.py:39
  439.8 13.8 %fusion = f32[512,512]{1,0:T(8,128)S(1)} fusion(bf16[8192,512]{1,0:T(8,128)(2,1)} %constant_dynamic-update-slice_fusion, bf16[64,8,64,128]{3,2,1,0:T(8,128)(2,1)} %bitcast.49), kind=kOutput, calls=%fused_computation | convolution fusion | flops 4294967296 | bytes 17825792 | tf_op jit(solution)/shard_map/dot_general | solution.py:41
  453.7 1.5 collective-permute-start.1
  455.2 8.4 %fusion.7 = bf16[4,64,128,128]{3,1,2,0:T(8,128)(2,1)} fusion(bf16[64,4,1,1,128,128]{5,4,1,3,2,0:T(8,128)(2,1)S(1)} %get-tuple-element.5, pred[8,64,64]{1,2,0:T(32,128)(4,1)S(1)} %iota_compare_fusion, s32[]{:T(128)S(6)} %select_n.14), kind=kOutput, calls=%fused_computation.9 | convolution fusion | flops 536870912 | bytes 16809988 | tf_op jit(solution)/shard_map/isab,isk->iakb/dot_general | solution.py:39
  463.6 12.9 %collective-permute-done.1 = f32[512,512]{1,0:T(8,128)S(1)} collective-permute-done((f32[512,512]{1,0:T(8,128)S(1)}, f32[512,512]{1,0:T(8,128)S(1)}, u32[]{:S(2)}, u32[]{:S(2)}) %collective-permute-start.1) | collective-permute-done | bytes 1048608 | tf_op jit(solution)/shard_map/ppermute | solution.py:44
  476.5 13.8 %fusion.20 = (f32[512]{0:T(512)S(1)}, f32[512,512]{1,0:T(8,128)S(1)}) fusion(f32[512,512]{1,0:T(8,128)S(1)} %collective-permute-done.1, bf16[8192,512]{1,0:T(8,128)(2,1)} %constant_dynamic-update-slice_fusion, bf16[64,8,64,128]{3,2,1,0:T(8,128)(2,1)} %bitcast.48), kind=kOutput, calls=%fused_computation.27 | convolution fusion | flops 4295753216 | bytes 18876416 | tf_op jit(solution)/shard_map/dot_general | solution.py:41
  490.3 10.4 %psum.7 = f32[512]{0:T(512)S(1)} all-reduce(f32[512]{0:T(512)S(1)} %get-tuple-element.7), channel_id=1, replica_groups=mesh['row'=2,'col'=64,'layer'=2] {'row','layer'}, use_global_device_ids=true, to_apply=%region_1.0 | all-reduce | flops 512 | bytes 4096 | tf_op jit(solution)/shard_map/psum | solution.py:48
  500.7 1.1 broadcast_divide_fusion
  (7 shorter events, 0.0 us)
Async XLA Ops:
  13.5 15.6 %copy-start.1 = (s32[8,1,1]{0,2,1:T(1,128)S(1)}, s32[8,1,1]{0,2,1:T(1,128)}, u32[]{:S(2)}) copy-start(s32[8,1,1]{0,2,1:T(1,128)} %param.3) | copy-start | bytes 100
  13.5 403.5 %all-to-all-start = ((bf16[64,8,1,1,128,128]{5,4,1,3,2,0:T(8,128)(2,1)}), bf16[64,8,1,1,128,128]{5,4,1,3,2,0:T(8,128)(2,1)}, u32[]{:S(2)}, u32[]{:S(2)}) async-start(bf16[64,8,1,1,128,128]{5,4,1,3,2,0:T(8,128)(2,1)} %stack.2), calls=%async_computation | async-start | bytes 33554432 | tf_op jit(solution)/shard_map/all_to_all | solution.py:28
  29.0 261.5 %all-gather.2.cloned.1.call-start = ((), (), s32[]{:S(2)}) async-start(), calls=%async_computation.1 | async-start | bytes 2129920 | tf_op jit(solution)/shard_map/all_gather | solution.py:24
  29.8 262.3 %collective-permute-start = (bf16[4096,512]{1,0:T(8,128)(2,1)}, bf16[4096,512]{1,0:T(8,128)(2,1)}, u32[]{:S(2)}, u32[]{:S(2)}) collective-permute-start(bf16[4096,512]{1,0:T(8,128)(2,1)} %bitcast.50), channel_id=1, source_target_pairs={{0,128},{128,0},{1,129},{129,1},{2,130},{130,2},{3,131},{131,3},{4... | collective-permute-start | bytes 12582920 | tf_op jit(solution)/shard_map/ppermute | solution.py:13
  30.8 4.2 copy-start
  453.7 22.9 %collective-permute-start.1 = (f32[512,512]{1,0:T(8,128)S(1)}, f32[512,512]{1,0:T(8,128)S(1)}, u32[]{:S(2)}, u32[]{:S(2)}) collective-permute-start(f32[512,512]{1,0:T(8,128)S(1)} %fusion), channel_id=1, source_target_pairs={{0,1},{1,0},{2,3},{3,2},{4,5},{5,4},{6,7},{7,6},{8,9},{9,8},{10,11... | collective-permute-start | bytes 3145736 | tf_op jit(solution)/shard_map/ppermute | solution.py:44
Sparse Core Ops, SparseCore 0:
  33.4 257.0 all-gather.1
